TPU v7x, 32 devices: a whole 2x2x4 slice. The times are simulated.
32 devices in a mesh: batch: 8 (over y, x, core), seq: 4 (over z).
Axes of the slice: x: 2, y: 2, z: 4, core: 2. Of those that a mesh axis runs over, the one named last changes fastest.
Arguments:
- query_rows: bfloat16 [8, 2560, 3072], P('batch', 'seq'), may hold values from -16 to 16
- key_rows: bfloat16 [8, 2560, 3072], P('batch', 'seq'), may hold values from -16 to 16
- value_rows: bfloat16 [8, 2560, 3072], P('batch', 'seq'), may hold values from -10 to 10
- cached_rows: bfloat16 [8, 2560, 3072], P('batch', 'seq'), may hold values from -4 to 4
- plan: int32 [8, 28], replicated, may hold values from 0 to 1, as said below
- timestep: int32 [8], replicated, may hold values from 0 to 27
- assignment: int32 [8], replicated, may hold values from 0 to 7, as said below
Outputs:
- refreshed: bfloat16 [8, 2560, 3072], P('batch', 'seq')
Inputs may be any that keep to these rules, and one draw needn't show every extreme that they name: plan[r, t] is 1 for t = 0 and for the timesteps at which request r refreshes, every 3 timesteps from its own offset, else 0. `assignment`: a permutation of the requests; of the two slots g and g + 4, exactly one holds a request with active = 1.
All inputs are finite; a program needn't handle non-finite values.
Results may differ from a plain program's by a relative error of at most 0.0025.
Values may be sent and summed in bfloat16 or wider, within the bound.
A program may use at most 128 MiB of HBM per device.

v0:
```python
import functools
import math

import jax
import jax.numpy as jnp
from jax import lax
from jax.experimental import pallas as pl
from jax.experimental.pallas import tpu as pltpu
from jax.sharding import PartitionSpec as P

HEAD_DIM = 128
MESH = pl.DeviceIdType.MESH
AHEAD = 3
PARTS = 2
SKEW = 4
LAG = 6
RETURN_LAG = 1


def block_rows(row_count):
    for candidate in range(512, row_count + 1):
        if row_count % candidate == 0:
            return candidate
    return row_count


def attend(head_queries, head_keys, head_values):
    row_count, head_count, depth = head_queries.shape
    block = block_rows(row_count)
    factor = 1.0 / math.sqrt(depth)
    stacked = head_queries.reshape(row_count // block, block, head_count, depth)

    def one_block(query_block):
        scores = (
            jnp.einsum("qnd,knd->nqk", query_block, head_keys, preferred_element_type=jnp.float32)
            * factor
        )
        peak = jnp.max(scores, axis=2, keepdims=True)
        shifted = jnp.exp(scores - peak)
        total = jnp.sum(shifted, axis=2)
        weights = shifted.astype(jnp.bfloat16)
        mixed = jnp.einsum("nqk,knd->qnd", weights, head_values, preferred_element_type=jnp.float32)
        return (mixed / jnp.transpose(total)[:, :, None]).astype(jnp.bfloat16)

    return lax.map(one_block, stacked).reshape(row_count, head_count, depth)


def skipped(head_queries, head_keys, head_values):
    return jnp.zeros(head_queries.shape, jnp.bfloat16)


def plain_body(query_rows, key_rows, value_rows, cached_rows, plan, timestep, assignment):
    pieces = lax.axis_size("seq")
    local_rows = query_rows.shape[1]
    width = query_rows.shape[2]
    group = lax.axis_index("batch")
    slot_index = jnp.arange(assignment.shape[0], dtype=jnp.int32)
    request = jnp.sum(jnp.where(slot_index == group, assignment, 0))
    moment = jnp.sum(jnp.where(slot_index == request, timestep, 0))
    step_index = jnp.arange(plan.shape[1], dtype=jnp.int32)
    chosen = (slot_index[:, None] == request) & (step_index[None, :] == moment)
    active = jnp.sum(jnp.where(chosen, plan, 0)) > 0

    def arrange(rows):
        return rows[0].reshape(local_rows, pieces, width // (pieces * HEAD_DIM), HEAD_DIM)

    def gather(rows):
        return lax.all_to_all(arrange(rows), "seq", split_axis=1, concat_axis=0, tiled=True)[:, 0]

    attended = lax.cond(
        active, attend, skipped, gather(query_rows), gather(key_rows), gather(value_rows)
    )
    moved = lax.all_to_all(attended[:, None], "seq", split_axis=0, concat_axis=1, tiled=True)
    fresh = moved.reshape(1, local_rows, width)
    return jnp.where(active, fresh, cached_rows)


def exclusive(number, other, size):
    total = 0
    bit = 1
    while bit < size:
        total = total + bit * ((number // bit + other // bit) % 2)
        bit *= 2
    return total


def kernel(
    groups, pieces, stages,
    assignment_ref, timestep_ref, plan_ref, query_ref, key_ref, value_ref,
    out_ref, flag_ref,
    own, paired, gathered, mixed,
    own_sem, pair_send, pair_recv, ring_send, ring_recv,
    back_send, back_recv, home_send, home_recv, local_sem,
):
    batch = lax.axis_index("batch")
    me = lax.axis_index("seq")
    half = groups // 2
    side = batch // half
    partner = (batch + half) % groups
    other_side = 1 - side
    rows = query_ref.shape[1]
    count = stages * pieces
    sources = (query_ref, key_ref, value_ref)

    request = assignment_ref[batch]
    moment = timestep_ref[request]
    active = plan_ref[request, moment] > 0
    flag_ref[0] = plan_ref[request, moment]

    def split(index):
        return index // pieces, pieces - 1 - index % pieces

    def columns(which, peer, stage):
        head = (which * pieces + peer) * stages + stage
        return pl.ds(pl.multiple_of(head * HEAD_DIM, HEAD_DIM), HEAD_DIM)

    def rows_of(peer):
        return pl.ds(pl.multiple_of(peer * rows, rows), rows)

    share = rows // PARTS

    def part_rows(part, peer=0):
        return pl.ds(pl.multiple_of(peer * rows + part * share, share), share)

    def pair_copy(index, kind):
        stage, offset = split(index)
        peer = exclusive(me, offset, pieces)
        return pltpu.make_async_remote_copy(
            src_ref=sources[kind].at[0, :, columns(other_side, peer, stage)],
            dst_ref=paired.at[kind, index],
            send_sem=pair_send.at[kind, index],
            recv_sem=pair_recv.at[kind, index],
            device_id=(partner, me),
            device_id_type=MESH,
        )

    def ring_copy(index, kind):
        stage, offset = split(index)
        peer = exclusive(me, offset, pieces)
        return pltpu.make_async_remote_copy(
            src_ref=paired.at[kind, index],
            dst_ref=gathered.at[kind, stage, rows_of(me)],
            send_sem=ring_send.at[kind, index],
            recv_sem=ring_recv.at[kind, index],
            device_id=(batch, peer),
            device_id_type=MESH,
        )

    def back_copy(index, part):
        stage, offset = split(index)
        peer = exclusive(me, offset, pieces)
        return pltpu.make_async_remote_copy(
            src_ref=mixed.at[stage, part_rows(part, peer)],
            dst_ref=out_ref.at[0, part_rows(part), columns(side, me, stage)],
            send_sem=back_send.at[index, part],
            recv_sem=back_recv.at[index, part],
            device_id=(batch, peer),
            device_id_type=MESH,
        )

    def home_copy(index, part):
        stage, offset = split(index)
        peer = exclusive(me, offset, pieces)
        return pltpu.make_async_remote_copy(
            src_ref=out_ref.at[0, part_rows(part), columns(side, peer, stage)],
            dst_ref=out_ref.at[0, part_rows(part), columns(side, peer, stage)],
            send_sem=home_send.at[index, part],
            recv_sem=home_recv.at[index, part],
            device_id=(partner, me),
            device_id_type=MESH,
        )

    def local_copy(index):
        stage, _ = split(index)
        return pltpu.make_async_copy(
            mixed.at[stage, rows_of(me)],
            out_ref.at[0, :, columns(side, me, stage)],
            local_sem.at[stage],
        )

    def own_copy(kind):
        width = pieces * stages * HEAD_DIM
        start = pl.multiple_of(side * width, HEAD_DIM)
        return pltpu.make_async_copy(
            sources[kind].at[0, :, pl.ds(start, width)], own.at[kind], own_sem.at[kind]
        )

    for kind in range(3):
        own_copy(kind).start()

    barrier = pltpu.get_barrier_semaphore()
    pl.semaphore_signal(barrier, inc=1, device_id=(partner, me), device_id_type=MESH)
    for step in range(1, pieces):
        pl.semaphore_signal(
            barrier, inc=1, device_id=(batch, (me + step) % pieces), device_id_type=MESH
        )
    pl.semaphore_wait(barrier, pieces)

    def start_pair(step):
        @pl.when(step < count)
        def _():
            for kind in (1, 2):
                pair_copy(step, kind).start()

        @pl.when((step >= SKEW) & (step < count + SKEW))
        def _():
            pair_copy(step - SKEW, 0).start()

    def first(step, carry):
        start_pair(step)
        return carry

    lax.fori_loop(0, AHEAD, first, 0)
    for kind in range(3):
        own_copy(kind).wait()

    def attention(index):
        stage, offset = split(index)
        peer = exclusive(me, offset, pieces)

        @pl.when(index % pieces == 0)
        def _():
            def arrived(step, carry):
                for kind in (1, 2):
                    ring_copy(stage * pieces + step, kind).wait_recv()
                return carry

            lax.fori_loop(0, pieces - 1, arrived, 0)

        @pl.when(offset != 0)
        def _():
            ring_copy(index, 0).wait_recv()

        keys = gathered[1, stage]
        values = gathered[2, stage]
        factor = math.log2(math.e) / math.sqrt(HEAD_DIM)

        def part_of(part, carry):
            where = part_rows(part, peer)
            queries = gathered[0, stage, where, :]
            scores = lax.dot_general(
                queries, keys, (((1,), (1,)), ((), ())), preferred_element_type=jnp.float32
            )
            peak = jnp.max(scores, axis=1, keepdims=True)
            weights = jnp.exp2((scores - peak) * factor)
            total = jnp.sum(weights, axis=1, keepdims=True)
            result = jnp.dot(
                weights.astype(jnp.bfloat16), values, preferred_element_type=jnp.float32
            )
            mixed[stage, where, :] = (result / total).astype(jnp.bfloat16)

            @pl.when(offset != 0)
            def _():
                back_copy(index, part).start()

            return carry

        lax.fori_loop(0, PARTS, part_of, 0)

    def pass_on(index, kind):
        stage, offset = split(index)
        peer = exclusive(me, offset, pieces)
        place = pl.multiple_of((peer * stages + stage) * HEAD_DIM, HEAD_DIM)
        pair_copy(index, kind).wait_recv()
        mine = own[kind, :, pl.ds(place, HEAD_DIM)]
        chosen = lax.select_n(active, paired[kind, index], mine)

        @pl.when(offset != 0)
        def _():
            paired[kind, index] = chosen
            ring_copy(index, kind).start()

        @pl.when(offset == 0)
        def _():
            gathered[kind, stage, rows_of(me), :] = chosen

    def step_of(step, carry):
        start_pair(step + AHEAD)

        @pl.when(step < count)
        def _():
            for kind in (1, 2):
                pass_on(step, kind)

        @pl.when((step >= SKEW) & (step < count + SKEW))
        def _():
            pass_on(step - SKEW, 0)

        block = step - LAG

        @pl.when((block >= 0) & (block < count))
        def _():
            attention(block)
            _, offset = split(block)

            @pl.when(offset == 0)
            def _():
                local_copy(block).start()

        returned = block - RETURN_LAG

        @pl.when(returned >= 0)
        def _():
            _, offset = split(returned)

            @pl.when(offset == 0)
            def _():
                local_copy(returned).wait()

            for part in range(PARTS):
                @pl.when(offset != 0)
                def _():
                    back_copy(returned, part).wait_recv()

                home_copy(returned, part).start()

        return carry

    lax.fori_loop(0, count + LAG + RETURN_LAG, step_of, 0)

    def finish(index, carry):
        _, offset = split(index)
        for kind in range(3):
            pair_copy(index, kind).wait_send()

        @pl.when(offset != 0)
        def _():
            for kind in range(3):
                ring_copy(index, kind).wait_send()
            for part in range(PARTS):
                back_copy(index, part).wait_send()

        for part in range(PARTS):
            home_copy(index, part).wait()
        return carry

    lax.fori_loop(0, count, finish, 0)


def paired_body(query_rows, key_rows, value_rows, cached_rows, plan, timestep, assignment):
    groups = lax.axis_size("batch")
    pieces = lax.axis_size("seq")
    _, rows, width = query_rows.shape
    stages = width // HEAD_DIM // (2 * pieces)
    count = stages * pieces
    smem = pl.BlockSpec(memory_space=pltpu.SMEM)
    anywhere = pl.BlockSpec(memory_space=pl.ANY)
    fresh, flag = pl.pallas_call(
        functools.partial(kernel, groups, pieces, stages),
        out_shape=(
            jax.ShapeDtypeStruct(query_rows.shape, jnp.bfloat16),
            jax.ShapeDtypeStruct((1,), jnp.int32),
        ),
        in_specs=[smem] * 3 + [anywhere] * 3,
        out_specs=(anywhere, smem),
        scratch_shapes=[
            pltpu.VMEM((3, rows, width // 2), jnp.bfloat16),
            pltpu.VMEM((3, count, rows, HEAD_DIM), jnp.bfloat16),
            pltpu.VMEM((3, stages, pieces * rows, HEAD_DIM), jnp.bfloat16),
            pltpu.VMEM((stages, pieces * rows, HEAD_DIM), jnp.bfloat16),
            pltpu.SemaphoreType.DMA((3,)),
            pltpu.SemaphoreType.DMA((3, count)),
            pltpu.SemaphoreType.DMA((3, count)),
            pltpu.SemaphoreType.DMA((3, count)),
            pltpu.SemaphoreType.DMA((3, count)),
            pltpu.SemaphoreType.DMA((count, PARTS)),
            pltpu.SemaphoreType.DMA((count, PARTS)),
            pltpu.SemaphoreType.DMA((count, PARTS)),
            pltpu.SemaphoreType.DMA((count, PARTS)),
            pltpu.SemaphoreType.DMA((stages,)),
        ],
        compiler_params=pltpu.CompilerParams(
            collective_id=0, has_side_effects=True, vmem_limit_bytes=56 << 20
        ),
    )(assignment, timestep, plan, query_rows, key_rows, value_rows)
    return jnp.where(flag[0] > 0, fresh, cached_rows)


def solution(mesh):
    placed = (
        P("batch", "seq", None),
        P("batch", "seq", None),
        P("batch", "seq", None),
        P("batch", "seq", None),
        P(),
        P(),
        P(),
    )
    groups, pieces = mesh.shape["batch"], mesh.shape["seq"]

    def body(query_rows, *rest):
        heads = query_rows.shape[2] // HEAD_DIM
        rows = query_rows.shape[1]
        even = groups % 2 == 0 and heads % (2 * pieces) == 0 and rows % (16 * PARTS) == 0
        power = pieces > 1 and pieces & (pieces - 1) == 0
        chosen = paired_body if even and power else plain_body
        return chosen(query_rows, *rest)

    return jax.shard_map(
        body, mesh=mesh, in_specs=placed, out_specs=P("batch", "seq", None), check_vma=False
    )
```

profile of v0, /device:TPU:0, one launch (start us, length us, event | category | flops | bytes accessed | tf_op | source)
XLA Modules:
  0.0 196.8 jit_solution(16455129501492371537)
XLA Ops:
  0.0 0.0 copy-start
  0.0 193.8 %shard_map.73 = (bf16[1,640,3072]{2,1,0:T(8,128)(2,1)}, s32[1]{0:T(128)}) custom-call(s32[8]{0:T(128)} %assignment_ref.1, s32[8]{0:T(128)} %timestep_ref.1, s32[8,28]{1,0:T(8,128)} %plan_ref.1, bf16[1,640,3072]{2,1,0:T(8,128)(2,1)} %query_ref.1, bf16[1,640,3072]{2,1,0:T(8,128)(2,1)} %key_ref.1, bf16[1,640,3072]{2,1,0:T(8,128)(2,1)} %value_ref.1), custom_call_target="tpu_custom_call" | custom-call | tf_op jit(solution)/shard_map/pallas_call | solution.py:348
  194.4 0.0 copy-done
  194.4 2.3 %broadcast_select_fusion = bf16[1,640,3072]{2,1,0:T(8,128)(2,1)} fusion(bf16[1,640,3072]{2,1,0:T(8,128)(2,1)} %get-tuple-element.8, bf16[1,640,3072]{2,1,0:T(8,128)(2,1)S(1)} %copy-done, pred[]{:T(512)} %bitcast), kind=kLoop, calls=%fused_computation | loop fusion | flops 1966080 | bytes 11796481 | tf_op jit(solution)/shard_map/jit(_where)/select_n | solution.py:376
Async XLA Ops:
  0.0 194.4 %copy-start = (bf16[1,640,3072]{2,1,0:T(8,128)(2,1)S(1)}, bf16[1,640,3072]{2,1,0:T(8,128)(2,1)}, u32[]{:S(2)}) copy-start(bf16[1,640,3072]{2,1,0:T(8,128)(2,1)} %param.10) | copy-start | bytes 11796484
where the time goes:
time: 200 us; the launch traced here: 197 us
  Pallas kernels  194 us (97%)
  other arithmetic  2.34 us (1%)
    pallas_call x1, Pallas kernels, paired_body(): pl.pallas_call(functools.partial(kernel, groups, pieces, stages), out_sha...  194 us

commit v1 on v0

v1 whole, which is shorter than its diff:
```python
import functools
import math

import jax
import jax.numpy as jnp
from jax import lax
from jax.experimental import pallas as pl
from jax.experimental.pallas import tpu as pltpu
from jax.sharding import PartitionSpec as P

HEAD_DIM = 128
MESH = pl.DeviceIdType.MESH
PARTS = 2
CUTS = 1
DELAY = 3
ORDER = ((1, 0), (2, 0), (1, 1), (2, 1), (0, 0), (0, 1))


def block_rows(row_count):
    for candidate in range(512, row_count + 1):
        if row_count % candidate == 0:
            return candidate
    return row_count


def attend(head_queries, head_keys, head_values):
    row_count, head_count, depth = head_queries.shape
    block = block_rows(row_count)
    factor = 1.0 / math.sqrt(depth)
    stacked = head_queries.reshape(row_count // block, block, head_count, depth)

    def one_block(query_block):
        scores = (
            jnp.einsum("qnd,knd->nqk", query_block, head_keys, preferred_element_type=jnp.float32)
            * factor
        )
        peak = jnp.max(scores, axis=2, keepdims=True)
        shifted = jnp.exp(scores - peak)
        total = jnp.sum(shifted, axis=2)
        weights = shifted.astype(jnp.bfloat16)
        mixed = jnp.einsum("nqk,knd->qnd", weights, head_values, preferred_element_type=jnp.float32)
        return (mixed / jnp.transpose(total)[:, :, None]).astype(jnp.bfloat16)

    return lax.map(one_block, stacked).reshape(row_count, head_count, depth)


def skipped(head_queries, head_keys, head_values):
    return jnp.zeros(head_queries.shape, jnp.bfloat16)


def plain_body(query_rows, key_rows, value_rows, cached_rows, plan, timestep, assignment):
    pieces = lax.axis_size("seq")
    local_rows = query_rows.shape[1]
    width = query_rows.shape[2]
    group = lax.axis_index("batch")
    slot_index = jnp.arange(assignment.shape[0], dtype=jnp.int32)
    request = jnp.sum(jnp.where(slot_index == group, assignment, 0))
    moment = jnp.sum(jnp.where(slot_index == request, timestep, 0))
    step_index = jnp.arange(plan.shape[1], dtype=jnp.int32)
    chosen = (slot_index[:, None] == request) & (step_index[None, :] == moment)
    active = jnp.sum(jnp.where(chosen, plan, 0)) > 0

    def arrange(rows):
        return rows[0].reshape(local_rows, pieces, width // (pieces * HEAD_DIM), HEAD_DIM)

    def gather(rows):
        return lax.all_to_all(arrange(rows), "seq", split_axis=1, concat_axis=0, tiled=True)[:, 0]

    attended = lax.cond(
        active, attend, skipped, gather(query_rows), gather(key_rows), gather(value_rows)
    )
    moved = lax.all_to_all(attended[:, None], "seq", split_axis=0, concat_axis=1, tiled=True)
    fresh = moved.reshape(1, local_rows, width)
    return jnp.where(active, fresh, cached_rows)


def exclusive(number, other, size):
    total = 0
    bit = 1
    while bit < size:
        total = total + bit * ((number // bit + other // bit) % 2)
        bit *= 2
    return total


def kernel(
    groups, pieces, stages,
    assignment_ref, timestep_ref, plan_ref, query_ref, key_ref, value_ref, cached_ref,
    out_ref,
    own, other, paired, gathered, mixed, backs, homes, cached,
    own_sem, other_sem, cached_sem, pair_send, pair_recv, ring_send, ring_recv,
    back_send, back_recv, home_send, home_recv,
):
    batch = lax.axis_index("batch")
    me = lax.axis_index("seq")
    half = groups // 2
    side = batch // half
    partner = (batch + half) % groups
    other_side = 1 - side
    rows = query_ref.shape[1]
    count = stages * pieces
    sources = (query_ref, key_ref, value_ref)

    request = assignment_ref[batch]
    moment = timestep_ref[request]
    active = plan_ref[request, moment] > 0

    def split(index):
        return index // pieces, pieces - 1 - index % pieces

    def columns(which, peer, stage):
        head = (which * pieces + peer) * stages + stage
        return pl.ds(pl.multiple_of(head * HEAD_DIM, HEAD_DIM), HEAD_DIM)

    def rows_of(peer):
        return pl.ds(pl.multiple_of(peer * rows, rows), rows)

    share = rows // PARTS
    slab = rows // CUTS

    def part_rows(part, peer=0):
        return pl.ds(pl.multiple_of(peer * rows + part * share, share), share)

    def cut_rows(cut, peer=0):
        return pl.ds(pl.multiple_of(peer * rows + cut * slab, slab), slab)

    def other_copy(index, kind):
        stage, offset = split(index)
        peer = exclusive(me, offset, pieces)
        return pltpu.make_async_copy(
            sources[kind].at[0, :, columns(other_side, peer, stage)],
            other.at[kind, index],
            other_sem.at[kind, index],
        )

    def pair_copy(index, kind, cut):
        return pltpu.make_async_remote_copy(
            src_ref=other.at[kind, index, cut_rows(cut)],
            dst_ref=paired.at[kind, index, cut_rows(cut)],
            send_sem=pair_send.at[kind, index, cut],
            recv_sem=pair_recv.at[kind, index, cut],
            device_id=(partner, me),
            device_id_type=MESH,
        )

    def ring_copy(index, kind, cut):
        stage, offset = split(index)
        peer = exclusive(me, offset, pieces)
        return pltpu.make_async_remote_copy(
            src_ref=paired.at[kind, index, cut_rows(cut)],
            dst_ref=gathered.at[kind, stage, cut_rows(cut, me)],
            send_sem=ring_send.at[kind, index, cut],
            recv_sem=ring_recv.at[kind, index, cut],
            device_id=(batch, peer),
            device_id_type=MESH,
        )

    def back_copy(index, part):
        stage, offset = split(index)
        peer = exclusive(me, offset, pieces)
        return pltpu.make_async_remote_copy(
            src_ref=mixed.at[stage, part_rows(part, peer)],
            dst_ref=backs.at[index, part_rows(part)],
            send_sem=back_send.at[index, part],
            recv_sem=back_recv.at[index, part],
            device_id=(batch, peer),
            device_id_type=MESH,
        )

    def home_copy(index, part):
        return pltpu.make_async_remote_copy(
            src_ref=backs.at[index, part_rows(part)],
            dst_ref=homes.at[index, part_rows(part)],
            send_sem=home_send.at[index, part],
            recv_sem=home_recv.at[index, part],
            device_id=(partner, me),
            device_id_type=MESH,
        )

    def settle(index, part, which, fresh):
        stage, offset = split(index)
        lanes = columns(which, exclusive(me, offset, pieces), stage)
        where = part_rows(part)
        out_ref[0, where, lanes] = lax.select_n(active, cached[where, lanes], fresh[index, where])

    def own_copy(kind):
        width = pieces * stages * HEAD_DIM
        start = pl.multiple_of(side * width, HEAD_DIM)
        return pltpu.make_async_copy(
            sources[kind].at[0, :, pl.ds(start, width)], own.at[kind], own_sem.at[kind]
        )

    barrier = pltpu.get_barrier_semaphore()
    pl.semaphore_signal(barrier, inc=1, device_id=(partner, me), device_id_type=MESH)
    for step in range(1, pieces):
        pl.semaphore_signal(
            barrier, inc=1, device_id=(batch, (me + step) % pieces), device_id_type=MESH
        )

    def load_others(group, carry):
        for kind, sub in ORDER:
            other_copy(2 * group + sub, kind).start()
        return carry

    lax.fori_loop(0, count // 2, load_others, 0)
    for kind in (1, 2, 0):
        own_copy(kind).start()
    pl.semaphore_wait(barrier, pieces)

    per_stage = 3 * pieces
    forwards = stages * per_stage
    stage_units = pieces * PARTS
    units = stages * stage_units
    start = per_stage + min(DELAY, 3 * pieces // 2)
    held_from = max(stages - 2, 0) * stage_units
    held_to = held_from + stage_units // 2 * (stages > 1)
    half_units = stage_units // 2
    lead = half_units // 2
    inner = (me + 1) // 2 % 2

    def start_pairs(group, carry):
        for kind, sub in ORDER:
            other_copy(2 * group + sub, kind).wait()
            for cut in range(CUTS):
                pair_copy(2 * group + sub, kind, cut).start()
        return carry

    start_pairs(0, 0)
    cached_copy = pltpu.make_async_copy(cached_ref.at[0], cached, cached_sem)
    cached_copy.start()
    for kind in range(3):
        own_copy(kind).wait()

    def forward(number):
        place = number % 6

        @pl.when((place == 0) & (number < forwards - 6))
        def _():
            start_pairs(number // 6 + 1, 0)

        late = place // 4
        kind = (1 - late) * (1 + place % 2)
        index = number // 6 * 2 + (1 - late) * (place // 2) + late * (place - 4)
        stage, offset = split(index)
        peer = exclusive(me, offset, pieces)
        lanes = pl.ds(pl.multiple_of((peer * stages + stage) * HEAD_DIM, HEAD_DIM), HEAD_DIM)
        for cut in range(CUTS):
            pair_copy(index, kind, cut).wait_recv()
            mine = own[kind, cut_rows(cut), lanes]
            chosen = lax.select_n(active, paired[kind, index, cut_rows(cut)], mine)

            @pl.when(offset != 0)
            def _():
                paired[kind, index, cut_rows(cut)] = chosen
                ring_copy(index, kind, cut).start()

            @pl.when(offset == 0)
            def _():
                gathered[kind, stage, cut_rows(cut, me), :] = chosen

    def send_back(unit, carry):
        index, part = unit // PARTS, unit % PARTS
        _, offset = split(index)

        @pl.when(offset != 0)
        def _():
            back_copy(index, part).start()

        return carry

    def unit_of(stage, place):
        crossing = place // half_units
        turned = (place + inner * (half_units // 2)) % half_units
        within = crossing * turned + (1 - crossing) * (half_units + place)
        unit = stage * stage_units + within
        return unit // PARTS, unit % PARTS

    def send_home(stage, place):
        index, part = unit_of(stage, place)
        _, offset = split(index)

        @pl.when(offset != 0)
        def _():
            back_copy(index, part).wait_recv()

        home_copy(index, part).start()
        settle(index, part, side, backs)

    def come_home(stage, place):
        index, part = unit_of(stage, place)
        home_copy(index, part).wait_recv()
        settle(index, part, other_side, homes)

    def each(first, number, low, high, action):
        span = high - low

        def body(item, carry):
            action(first + item // span, low + item % span)
            return carry

        lax.fori_loop(0, number * span, body, 0)

    def attention(unit, carry):
        index, part = unit // PARTS, unit % PARTS
        stage, offset = split(index)
        peer = exclusive(me, offset, pieces)

        @pl.when((unit % stage_units == 0) & (stage > 0))
        def _():
            each(stage - 1, 1, 0, half_units, send_home)

        @pl.when(unit % stage_units == 0)
        def _():
            def arrived(step, carry):
                for kind in (1, 2):
                    for cut in range(CUTS):
                        ring_copy(stage * pieces + step, kind, cut).wait_recv()
                return carry

            lax.fori_loop(0, pieces - 1, arrived, 0)

            @pl.when((unit == units - stage_units) & (inner == 0))
            def _():
                lax.fori_loop(held_from, held_to, send_back, 0)

        @pl.when((offset != 0) & (part == 0))
        def _():
            for cut in range(CUTS):
                ring_copy(index, 0, cut).wait_recv()

        factor = math.log2(math.e) / math.sqrt(HEAD_DIM)
        where = part_rows(part, peer)
        queries = gathered[0, stage, where, :]
        scores = lax.dot_general(
            queries, gathered[1, stage], (((1,), (1,)), ((), ())),
            preferred_element_type=jnp.float32,
        )
        peak = jnp.max(scores, axis=1, keepdims=True)
        weights = jnp.exp2((scores - peak) * factor)
        total = jnp.sum(weights, axis=1, keepdims=True)
        result = jnp.dot(
            weights.astype(jnp.bfloat16), gathered[2, stage], preferred_element_type=jnp.float32
        )
        blended = (result / total).astype(jnp.bfloat16)

        @pl.when(offset != 0)
        def _():
            mixed[stage, where, :] = blended

        @pl.when(offset == 0)
        def _():
            backs[index, part_rows(part)] = blended

        @pl.when((unit < held_from) | (unit >= held_to))
        def _():
            send_back(unit, 0)

        spot = unit % stage_units

        @pl.when((stage > 0) & (spot >= half_units) & (unit < units - lead))
        def _():
            send_home(stage - 1, spot)

        return carry

    def early(number, carry):
        forward(number)
        return carry

    lax.fori_loop(0, min(start, forwards), early, 0)
    cached_copy.wait()

    def step_of(number, carry):
        @pl.when(number < forwards)
        def _():
            forward(number)

        done = number - start
        lax.fori_loop(done * PARTS // 3, (done + 1) * PARTS // 3, attention, 0)

        @pl.when((number == forwards - 1) & (inner == 1))
        def _():
            lax.fori_loop(held_from, held_to, send_back, 0)

        return carry

    lax.fori_loop(start, start + forwards, step_of, 0)
    def inputs_sent(index, carry):
        _, offset = split(index)
        for kind in range(3):
            for cut in range(CUTS):
                pair_copy(index, kind, cut).wait_send()

        @pl.when(offset != 0)
        def _():
            for kind in range(3):
                for cut in range(CUTS):
                    ring_copy(index, kind, cut).wait_send()

        return carry

    def outputs_sent(index, carry):
        _, offset = split(index)
        for part in range(PARTS):
            home_copy(index, part).wait_send()

        @pl.when(offset != 0)
        def _():
            for part in range(PARTS):
                back_copy(index, part).wait_send()

        return carry

    outer = half_units + lead
    final = stages - 1
    few = max(final - 1, 0)
    each(final, 1, 0, half_units, send_home)
    each(final, 1, half_units, outer, send_home)
    lax.fori_loop(0, count, inputs_sent, 0)
    each(0, few, 0, stage_units, come_home)
    each(few, final - few, 0, outer, come_home)
    each(few, final - few, outer, stage_units, send_home)
    each(final, 1, 0, half_units, come_home)
    each(final, 1, outer, stage_units, send_home)
    each(final, 1, half_units, outer, come_home)
    each(few, stages - few, outer, stage_units, come_home)
    lax.fori_loop(0, count, outputs_sent, 0)


def paired_body(query_rows, key_rows, value_rows, cached_rows, plan, timestep, assignment):
    groups = lax.axis_size("batch")
    pieces = lax.axis_size("seq")
    _, rows, width = query_rows.shape
    stages = width // HEAD_DIM // (2 * pieces)
    count = stages * pieces
    smem = pl.BlockSpec(memory_space=pltpu.SMEM)
    anywhere = pl.BlockSpec(memory_space=pl.ANY)
    block = (rows, HEAD_DIM)
    return pl.pallas_call(
        functools.partial(kernel, groups, pieces, stages),
        out_shape=pltpu.VMEM(query_rows.shape, jnp.bfloat16),
        in_specs=[smem] * 3 + [anywhere] * 4,
        out_specs=pl.BlockSpec(memory_space=pltpu.VMEM),
        scratch_shapes=[
            pltpu.VMEM((3, rows, width // 2), jnp.bfloat16),
            pltpu.VMEM((3, count) + block, jnp.bfloat16),
            pltpu.VMEM((3, count) + block, jnp.bfloat16),
            pltpu.VMEM((3, stages, pieces * rows, HEAD_DIM), jnp.bfloat16),
            pltpu.VMEM((stages, pieces * rows, HEAD_DIM), jnp.bfloat16),
            pltpu.VMEM((count,) + block, jnp.bfloat16),
            pltpu.VMEM((count,) + block, jnp.bfloat16),
            pltpu.VMEM((rows, width), jnp.bfloat16),
            pltpu.SemaphoreType.DMA((3,)),
            pltpu.SemaphoreType.DMA((3, count)),
            pltpu.SemaphoreType.DMA,
            pltpu.SemaphoreType.DMA((3, count, CUTS)),
            pltpu.SemaphoreType.DMA((3, count, CUTS)),
            pltpu.SemaphoreType.DMA((3, count, CUTS)),
            pltpu.SemaphoreType.DMA((3, count, CUTS)),
            pltpu.SemaphoreType.DMA((count, PARTS)),
            pltpu.SemaphoreType.DMA((count, PARTS)),
            pltpu.SemaphoreType.DMA((count, PARTS)),
            pltpu.SemaphoreType.DMA((count, PARTS)),
        ],
        compiler_params=pltpu.CompilerParams(
            collective_id=0, has_side_effects=True, vmem_limit_bytes=56 << 20
        ),
    )(assignment, timestep, plan, query_rows, key_rows, value_rows, cached_rows)


def solution(mesh):
    placed = (
        P("batch", "seq", None),
        P("batch", "seq", None),
        P("batch", "seq", None),
        P("batch", "seq", None),
        P(),
        P(),
        P(),
    )
    groups, pieces = mesh.shape["batch"], mesh.shape["seq"]

    def body(query_rows, *rest):
        heads = query_rows.shape[2] // HEAD_DIM
        rows = query_rows.shape[1]
        even = groups % 2 == 0 and heads % (2 * pieces) == 0 and rows % (16 * PARTS * CUTS) == 0
        power = pieces > 1 and pieces & (pieces - 1) == 0
        chosen = paired_body if even and power else plain_body
        return chosen(query_rows, *rest)

    return jax.shard_map(
        body, mesh=mesh, in_specs=placed, out_specs=P("batch", "seq", None), check_vma=False
    )
```

time: 200 us -> 195 us (0.975); the launches traced: 197 us -> 195 us
  other arithmetic: 2.34 us -> 0 us
    select_n x1 -> x0, other arithmetic: 2.34 us -> none  [paired_body(): return jnp.where(flag[0] > 0, fresh, cached_rows)]
where the time goes in v1:
time: 195 us
  Pallas kernels  193 us (99%)
    pallas_call x1, Pallas kernels, paired_body(): pl.pallas_call(functools.partial(kernel, groups, pieces, stages), out_sha...  193 us

profile of v1, /device:TPU:0, one launch (start us, length us, event | category | flops | bytes accessed | tf_op | source)
XLA Modules:
  0.0 195.3 jit_solution(4709600738449546292)
XLA Ops:
  0.0 193.4 %shard_map.73 = bf16[1,640,3072]{2,1,0:T(8,128)(2,1)S(1)} custom-call(s32[8]{0:T(128)} %assignment_ref.1, s32[8]{0:T(128)} %timestep_ref.1, s32[8,28]{1,0:T(8,128)} %plan_ref.1, bf16[1,640,3072]{2,1,0:T(8,128)(2,1)} %query_ref.1, bf16[1,640,3072]{2,1,0:T(8,128)(2,1)} %key_ref.1, bf16[1,640,3072]{2,1,0:T(8,128)(2,1)} %value_ref.1, ...), custom_call_target="tpu_custom_call" | custom-call | tf_op jit(solution)/shard_map/pallas_call | solution.py:439
  193.4 1.9 copy.9

commit v2 on v1

--- a/solution.py
+++ b/solution.py
@@ -211,7 +211,7 @@
     forwards = stages * per_stage
     stage_units = pieces * PARTS
     units = stages * stage_units
-    start = per_stage + min(DELAY, 3 * pieces // 2)
+    start = per_stage + min(DELAY, 3 * (pieces // 2 - 1))
     held_from = max(stages - 2, 0) * stage_units
     held_to = held_from + stage_units // 2 * (stages > 1)
     half_units = stage_units // 2
@@ -301,13 +301,14 @@
         lax.fori_loop(0, number * span, body, 0)
 
     def attention(unit, carry):
-        index, part = unit // PARTS, unit % PARTS
+        turn, part = unit // PARTS, unit % PARTS
+        index = turn // pieces * pieces + (turn + pieces - 1) % pieces
         stage, offset = split(index)
         peer = exclusive(me, offset, pieces)
 
         @pl.when((unit % stage_units == 0) & (stage > 0))
         def _():
-            each(stage - 1, 1, 0, half_units, send_home)
+            each(stage - 1, 1, 0, half_units - PARTS, send_home)
 
         @pl.when(unit % stage_units == 0)
         def _():
@@ -350,16 +351,22 @@
         @pl.when(offset == 0)
         def _():
             backs[index, part_rows(part)] = blended
-
-        @pl.when((unit < held_from) | (unit >= held_to))
-        def _():
-            send_back(unit, 0)
+            home_copy(index, part).start()
+            settle(index, part, side, backs)
+
+        @pl.when((stage != stages - 2) | (offset < pieces // 2))
+        def _():
+            send_back(index * PARTS + part, 0)
 
         spot = unit % stage_units
 
         @pl.when((stage > 0) & (spot >= half_units) & (unit < units - lead))
         def _():
             send_home(stage - 1, spot)
+
+        @pl.when(unit >= units - lead)
+        def _():
+            send_home(stage, spot - lead)
 
         return carry
 
@@ -414,15 +421,14 @@
     outer = half_units + lead
     final = stages - 1
     few = max(final - 1, 0)
-    each(final, 1, 0, half_units, send_home)
-    each(final, 1, half_units, outer, send_home)
+    each(final, 1, 0, half_units - PARTS, send_home)
     lax.fori_loop(0, count, inputs_sent, 0)
     each(0, few, 0, stage_units, come_home)
     each(few, final - few, 0, outer, come_home)
     each(few, final - few, outer, stage_units, send_home)
-    each(final, 1, 0, half_units, come_home)
+    each(final, 1, half_units - PARTS, outer, come_home)
     each(final, 1, outer, stage_units, send_home)
-    each(final, 1, half_units, outer, come_home)
+    each(final, 1, 0, half_units - PARTS, come_home)
     each(few, stages - few, outer, stage_units, come_home)
     lax.fori_loop(0, count, outputs_sent, 0)
 

time: 195 us -> 191 us (0.979)
  Pallas kernels: 193 us -> 188 us
    pallas_call x1, Pallas kernels: 193 us -> 188 us  [paired_body(): pl.pallas_call(functools.partial(kernel, groups, pieces, stages), out_sha...]
where the time goes in v2:
time: 191 us; the launch traced here: 190 us
  Pallas kernels  188 us (98%)
  local copies, waits for them, and re-layouts  1.93 us (1%)
    pallas_call x1, Pallas kernels, paired_body(): pl.pallas_call(functools.partial(kernel, groups, pieces, stages), out_sha...  188 us

profile of v2, /device:TPU:0, one launch (start us, length us, event | category | flops | bytes accessed | tf_op | source)
XLA Modules:
  0.0 190.4 jit_solution(17028633628217036323)
XLA Ops:
  0.0 188.4 %shard_map.73 = bf16[1,640,3072]{2,1,0:T(8,128)(2,1)S(1)} custom-call(s32[8]{0:T(128)} %assignment_ref.1, s32[8]{0:T(128)} %timestep_ref.1, s32[8,28]{1,0:T(8,128)} %plan_ref.1, bf16[1,640,3072]{2,1,0:T(8,128)(2,1)} %query_ref.1, bf16[1,640,3072]{2,1,0:T(8,128)(2,1)} %key_ref.1, bf16[1,640,3072]{2,1,0:T(8,128)(2,1)} %value_ref.1, ...), custom_call_target="tpu_custom_call" | custom-call | tf_op jit(solution)/shard_map/pallas_call | solution.py:445
  188.4 1.9 %copy.9 = bf16[1,640,3072]{2,1,0:T(8,128)(2,1)} copy(bf16[1,640,3072]{2,1,0:T(8,128)(2,1)S(1)} %shard_map.73) | data formatting | bytes 7864320

commit v3 on v2

--- a/solution.py
+++ b/solution.py
@@ -10,7 +10,7 @@
 
 HEAD_DIM = 128
 MESH = pl.DeviceIdType.MESH
-PARTS = 2
+PARTS = 4
 CUTS = 1
 DELAY = 3
 ORDER = ((1, 0), (2, 0), (1, 1), (2, 1), (0, 0), (0, 1))
@@ -422,10 +422,10 @@
     final = stages - 1
     few = max(final - 1, 0)
     each(final, 1, 0, half_units - PARTS, send_home)
+    each(few, final - few, outer, stage_units, send_home)
     lax.fori_loop(0, count, inputs_sent, 0)
     each(0, few, 0, stage_units, come_home)
     each(few, final - few, 0, outer, come_home)
-    each(few, final - few, outer, stage_units, send_home)
     each(final, 1, half_units - PARTS, outer, come_home)
     each(final, 1, outer, stage_units, send_home)
     each(final, 1, 0, half_units - PARTS, come_home)

time: 191 us -> 189 us (0.990)
  no operation moved by 1% of the time
where the time goes in v3:
time: 189 us
  Pallas kernels  187 us (99%)
  local copies, waits for them, and re-layouts  1.93 us (1%)
    pallas_call x1, Pallas kernels, paired_body(): pl.pallas_call(functools.partial(kernel, groups, pieces, stages), out_sha...  187 us

profile of v3, /device:TPU:0, one launch (start us, length us, event | category | flops | bytes accessed | tf_op | source)
XLA Modules:
  0.0 188.9 jit_solution(9931801930234061828)
XLA Ops:
  0.0 186.9 %shard_map.73 = bf16[1,640,3072]{2,1,0:T(8,128)(2,1)S(1)} custom-call(s32[8]{0:T(128)} %assignment_ref.1, s32[8]{0:T(128)} %timestep_ref.1, s32[8,28]{1,0:T(8,128)} %plan_ref.1, bf16[1,640,3072]{2,1,0:T(8,128)(2,1)} %query_ref.1, bf16[1,640,3072]{2,1,0:T(8,128)(2,1)} %key_ref.1, bf16[1,640,3072]{2,1,0:T(8,128)(2,1)} %value_ref.1, ...), custom_call_target="tpu_custom_call" | custom-call | tf_op jit(solution)/shard_map/pallas_call | solution.py:445
  186.9 1.9 %copy.9 = bf16[1,640,3072]{2,1,0:T(8,128)(2,1)} copy(bf16[1,640,3072]{2,1,0:T(8,128)(2,1)S(1)} %shard_map.73) | data formatting | bytes 7864320

commit v4 on v3

--- a/solution.py
+++ b/solution.py
@@ -426,8 +426,8 @@
     lax.fori_loop(0, count, inputs_sent, 0)
     each(0, few, 0, stage_units, come_home)
     each(few, final - few, 0, outer, come_home)
+    each(final, 1, outer, stage_units, send_home)
     each(final, 1, half_units - PARTS, outer, come_home)
-    each(final, 1, outer, stage_units, send_home)
     each(final, 1, 0, half_units - PARTS, come_home)
     each(few, stages - few, outer, stage_units, come_home)
     lax.fori_loop(0, count, outputs_sent, 0)

time: 189 us -> 189 us (level)
  no operation moved by 1% of the time
where the time goes in v4:
time: 189 us
  Pallas kernels  187 us (99%)
  local copies, waits for them, and re-layouts  1.93 us (1%)
    pallas_call x1, Pallas kernels, paired_body(): pl.pallas_call(functools.partial(kernel, groups, pieces, stages), out_sha...  187 us

profile of v4, /device:TPU:0, one launch (start us, length us, event | category | flops | bytes accessed | tf_op | source)
XLA Modules:
  0.0 188.9 jit_solution(10889373285140095274)
XLA Ops:
  0.0 186.9 %shard_map.73 = bf16[1,640,3072]{2,1,0:T(8,128)(2,1)S(1)} custom-call(s32[8]{0:T(128)} %assignment_ref.1, s32[8]{0:T(128)} %timestep_ref.1, s32[8,28]{1,0:T(8,128)} %plan_ref.1, bf16[1,640,3072]{2,1,0:T(8,128)(2,1)} %query_ref.1, bf16[1,640,3072]{2,1,0:T(8,128)(2,1)} %key_ref.1, bf16[1,640,3072]{2,1,0:T(8,128)(2,1)} %value_ref.1, ...), custom_call_target="tpu_custom_call" | custom-call | tf_op jit(solution)/shard_map/pallas_call | solution.py:445
  186.9 1.9 %copy.9 = bf16[1,640,3072]{2,1,0:T(8,128)(2,1)} copy(bf16[1,640,3072]{2,1,0:T(8,128)(2,1)S(1)} %shard_map.73) | data formatting | bytes 7864320
